TPU v7x, 32 devices: a whole 2x2x4 slice. The times are simulated.
32 devices in a mesh: series: 4 (over z), head: 8 (over y, x, core).
Axes of the slice: x: 2, y: 2, z: 4, core: 2. Of those that a mesh axis runs over, the one named last changes fastest.
Arguments:
- teacher_in: bfloat16 [32, 128, 4096], P(('series', 'head')), may hold values from -6 to 6
- teacher_gain: float32 [4096], replicated, may hold values from 0.5 to 1.5
- w_gate: bfloat16 [4096, 8192], P(None, 'head'), may hold values from -0.09375 to 0.09375
- w_up: bfloat16 [4096, 8192], P(None, 'head'), may hold values from -0.09375 to 0.09375
- readout: bfloat16 [8192, 1024], P('head'), may hold values from -0.0625 to 0.0625
- distill_proj: bfloat16 [4096, 1024], P('head'), may hold values from -0.09375 to 0.09375
- building_ids: int32 [32], P(('series', 'head')), may hold values from 0 to 1023
- student_in: bfloat16 [32, 128, 1024], P(('series', 'head')), may hold values from -6 to 6
- embed_rows: bfloat16 [1024, 1024], replicated, may hold values from -4 to 4
- covariates: bfloat16 [1024, 128], replicated, may hold values from -5 to 5
- cov_proj: bfloat16 [128, 1024], replicated, may hold values from -0.5 to 0.5
- student_gain: float32 [1024], replicated, may hold values from 0.25 to 1.75
- w_x: bfloat16 [1024, 2048], replicated, may hold values from -0.1875 to 0.1875
- w_bcdt: bfloat16 [1024, 288], replicated, may hold values from -0.1875 to 0.1875
- conv_w: float32 [4, 2304], replicated, may hold values from -3 to 3
- dt_bias: float32 [32], replicated, may hold values from -1 to 1
- a_log: float32 [32], replicated, may hold values from -6 to -2.5
- d_skip: float32 [32], replicated, may hold values from 0.5 to 1.5
- norm_gain: float32 [2048], replicated, may hold values from 0.25 to 1.75
- w_out: bfloat16 [2048, 1024], replicated, may hold values from -0.125 to 0.125
Outputs:
- grad_bcdt: float32 [1024, 288], P(('series', 'head'))
- grad_conv: float32 [4, 2304], P(None, ('series', 'head'))
- grad_gain: float32 [2048], P(('series', 'head'))
- grad_out: float32 [2048, 1024], P(('series', 'head'))
Inputs may be any that keep to these rules, and one draw needn't show every extreme that they name: `building_ids`: building ids index rows of the building tables.
All inputs are finite; a program needn't handle non-finite values.
Results may differ from a plain program's by a relative error of at most 0.013.
The roundings to bfloat16 on the way count: a program that leaves them out, or rounds other values in their place, can miss the bound.
Values may be sent and summed in bfloat16 or wider, within the bound.
No kernel may reach another device: no remote copies, remote signals or barrier semaphores. Data moves between devices by JAX's collectives and lax.ppermute only.
A program may use at most 128 MiB of HBM per device.

v0:
```python
from functools import partial
import jax
import jax.numpy as jnp
from jax import lax
from jax.sharding import PartitionSpec as P

EPS = 1e-05


def rms_scale(values, gain):
    mean_sq = jnp.mean(values * values, axis=-1, keepdims=True)
    return values * lax.rsqrt(mean_sq + EPS) * gain


def teacher_rows(row_block, teacher_gain, w_gate, w_up, readout, proj_rows, feat_start):
    normed = rms_scale(row_block.astype(jnp.float32), teacher_gain).astype(jnp.bfloat16)
    gate_vals = jnp.dot(normed, w_gate, preferred_element_type=jnp.float32)
    upward = jnp.dot(normed, w_up, preferred_element_type=jnp.float32)
    hidden = (jax.nn.silu(gate_vals) * upward).astype(jnp.bfloat16)
    features = lax.dynamic_slice_in_dim(row_block, feat_start, proj_rows.shape[0], 1)
    return jnp.dot(hidden, readout, preferred_element_type=jnp.float32) + jnp.dot(
        features, proj_rows, preferred_element_type=jnp.float32
    )


def mixer_core(projected, conv_w, norm_gain, x_stream, dt_bias, a_log, d_skip):
    seq_len = x_stream.shape[0]
    inner_width = x_stream.shape[1]
    head_count = dt_bias.shape[0]
    state_size = (projected.shape[1] - head_count) // 2
    head_size = inner_width // head_count
    mixture = jnp.concatenate([x_stream, projected[:, : 2 * state_size]], axis=1)
    taps = conv_w.shape[0]
    padded = jnp.pad(mixture, ((taps - 1, 0), (0, 0)))
    convolved = padded[0:seq_len] * conv_w[0]
    for offset in range(1, taps):
        convolved = convolved + padded[offset : offset + seq_len] * conv_w[offset]
    activated = jax.nn.silu(convolved)
    x_heads = activated[:, :inner_width].reshape(seq_len, head_count, head_size)
    b_state = activated[:, inner_width : inner_width + state_size]
    c_state = activated[:, inner_width + state_size :]
    dt_step = jax.nn.softplus(projected[:, 2 * state_size :] + dt_bias)
    running = jnp.cumsum(dt_step * -jnp.exp(a_log), axis=0)
    later_pos = lax.broadcasted_iota(jnp.int32, (seq_len, seq_len), 0)
    earlier_pos = lax.broadcasted_iota(jnp.int32, (seq_len, seq_len), 1)
    differences = running[:, None, :] - running[None, :, :]
    decays = jnp.exp(jnp.where((later_pos >= earlier_pos)[:, :, None], differences, -1e30))
    scores = jnp.dot(c_state, b_state.T, precision=lax.Precision.HIGHEST)
    weights = scores[:, :, None] * decays * dt_step[None, :, :]
    mixed = (
        jnp.einsum("tsh,shp->thp", weights, x_heads, precision=lax.Precision.HIGHEST)
        + d_skip[None, :, None] * x_heads
    )
    return rms_scale(mixed.reshape(seq_len, inner_width), norm_gain)


def student_terms(
    series_x,
    extra_row,
    target_rows,
    student_gain,
    w_x,
    w_bcdt,
    conv_w,
    dt_bias,
    a_log,
    d_skip,
    norm_gain,
    w_out,
    series_total,
):
    base = series_x.astype(jnp.float32) + extra_row[None, :]
    normed = rms_scale(base, student_gain).astype(jnp.bfloat16)
    x_stream = jnp.dot(normed, w_x, preferred_element_type=jnp.float32)
    projected = jnp.dot(normed, w_bcdt, preferred_element_type=jnp.float32)

    def forward(proj_in, conv_in, gain_in):
        return mixer_core(proj_in, conv_in, gain_in, x_stream, dt_bias, a_log, d_skip)

    out_norm, pullback = jax.vjp(forward, projected, conv_w, norm_gain)
    rounded = out_norm.astype(jnp.bfloat16)
    output = jnp.dot(rounded, w_out, preferred_element_type=jnp.float32)
    d_output = ((output - target_rows) / series_total).astype(jnp.bfloat16)
    d_norm = jnp.dot(d_output, w_out.T, preferred_element_type=jnp.float32)
    d_proj, g_conv, g_gain = pullback(d_norm)
    g_out = jnp.dot(rounded.T, d_output, preferred_element_type=jnp.float32)
    g_bcdt = jnp.dot(normed.T, d_proj.astype(jnp.bfloat16), preferred_element_type=jnp.float32)
    return (g_bcdt, g_conv, g_gain, g_out)


def per_device(
    teacher_in,
    teacher_gain,
    w_gate,
    w_up,
    readout,
    distill_proj,
    building_ids,
    student_in,
    embed_rows,
    covariates,
    cov_proj,
    student_gain,
    w_x,
    w_bcdt,
    conv_w,
    dt_bias,
    a_log,
    d_skip,
    norm_gain,
    w_out,
):
    own_series = teacher_in.shape[0]
    seq_len = teacher_in.shape[1]
    model_width = teacher_in.shape[2]
    series_total = own_series * lax.axis_size("series") * lax.axis_size("head")
    feat_start = lax.axis_index("head") * distill_proj.shape[0]
    row_block = lax.all_gather(teacher_in, "head", axis=0, tiled=True)
    count = row_block.shape[0]
    flat_rows = row_block.reshape(count * seq_len, model_width)
    terms = teacher_rows(flat_rows, teacher_gain, w_gate, w_up, readout, distill_proj, feat_start)
    group_terms = terms.reshape(count, seq_len, terms.shape[1])
    summed = lax.psum(group_terms, "head")
    target = lax.dynamic_slice_in_dim(summed, lax.axis_index("head") * own_series, own_series, 0)
    selector = (
        building_ids[:, None]
        == lax.broadcasted_iota(jnp.int32, (own_series, embed_rows.shape[0]), 1)
    ).astype(jnp.bfloat16)
    embedded = jnp.dot(selector, embed_rows, preferred_element_type=jnp.float32)
    cov_rows = jnp.dot(selector, covariates, preferred_element_type=jnp.float32).astype(
        jnp.bfloat16
    )
    extra = embedded + jnp.dot(cov_rows, cov_proj, preferred_element_type=jnp.float32)
    local_terms = partial(
        student_terms,
        student_gain=student_gain,
        w_x=w_x,
        w_bcdt=w_bcdt,
        conv_w=conv_w,
        dt_bias=dt_bias,
        a_log=a_log,
        d_skip=d_skip,
        norm_gain=norm_gain,
        w_out=w_out,
        series_total=series_total,
    )
    per_series = jax.vmap(local_terms)(student_in, extra, target)
    g_bcdt = jnp.sum(per_series[0], axis=0)
    g_conv = jnp.sum(per_series[1], axis=0)
    g_gain = jnp.sum(per_series[2], axis=0)
    g_out = jnp.sum(per_series[3], axis=0)
    g_bcdt, g_conv, g_gain, g_out = (
        lax.psum_scatter(g_bcdt, ("series", "head"), scatter_dimension=0, tiled=True),
        lax.psum_scatter(g_conv, ("series", "head"), scatter_dimension=1, tiled=True),
        lax.psum_scatter(g_gain, ("series", "head"), scatter_dimension=0, tiled=True),
        lax.psum_scatter(g_out, ("series", "head"), scatter_dimension=0, tiled=True),
    )
    return (g_bcdt, g_conv, g_gain, g_out)


def solution(mesh):
    return jax.shard_map(
        per_device,
        mesh=mesh,
        in_specs=(
            P(("series", "head"), None, None),
            P(),
            P(None, "head"),
            P(None, "head"),
            P("head", None),
            P("head", None),
            P(("series", "head")),
            P(("series", "head"), None, None),
            P(),
            P(),
            P(),
            P(),
            P(),
            P(),
            P(),
            P(),
            P(),
            P(),
            P(),
            P(),
        ),
        out_specs=(
            P(("series", "head"), None),
            P(None, ("series", "head")),
            P(("series", "head")),
            P(("series", "head"), None),
        ),
        check_vma=False,
    )
```

profile of v0, /device:TPU:0, one launch (start us, length us, event | category | flops | bytes accessed | tf_op | source)
XLA Modules:
  0.0 478.3 jit_solution(16399168680379305801)
XLA Ops:
  10.0 2.0 fusion.57
  13.8 3.0 convolution_bitcast_fusion
  16.8 50.2 %all-gather.2.cloned.1.call-done = bf16[8,128,4096]{2,1,0:T(8,128)(2,1)} async-done(((bf16[1,128,4096]{2,1,0:T(8,128)(2,1)}), bf16[8,128,4096]{2,1,0:T(8,128)(2,1)}) %all-gather.2.cloned.1.call-update) | async-done | bytes 8388624 | tf_op jit(solution)/shard_map/all_gather | solution.py:118
  67.1 5.2 %multiply_reduce_fusion = f32[8,128]{1,0:T(8,128)S(1)} fusion(bf16[8,128,4096]{2,1,0:T(8,128)(2,1)} %all-gather.2.cloned.1.call-done), kind=kLoop, calls=%fused_computation.1 | loop fusion | flops 12581888 | bytes 8392704 | tf_op jit(solution)/shard_map/reduce_sum | solution.py:11
  72.8 12.7 %fusion = f32[1024,1024]{1,0:T(8,128)} fusion(bf16[4096,1024]{1,0:T(8,128)(2,1)} %param.23, bf16[1024,4096]{1,0:T(8,128)(2,1)S(1)} %bitcast.132, f32[4096]{0:T(1024)} %param.21, f32[1024]{0:T(1024)S(1)} %rsqrt_bitcast_fusion), kind=kOutput, calls=%fused_computation.4 | convolution fusion | flops 8606711808 | bytes 20992000 | tf_op jit(solution)/shard_map/dot_general | solution.py:18
  85.5 18.4 %fusion.2 = f32[1024,1024]{1,0:T(8,128)} fusion(bf16[1024,1024]{1,0:T(8,128)(2,1)S(1)} %copy-done, f32[1024,1024]{1,0:T(8,128)} %fusion, bf16[4096,1024]{1,0:T(8,128)(2,1)} %param.22, bf16[1024,4096]{1,0:T(8,128)(2,1)} %bitcast.130, f32[4096]{0:T(1024)} %param.21, f32[1024]{0:T(1024)S(1)} %rsqrt_bitcast_fusion), kind=kOutput, calls=%fused_computation.6 | convolution fusion | flops 10760486912 | bytes 27283456 | tf_op jit(solution)/shard_map/dot_general | solution.py:21
  103.9 6.1 %convolution_add_fusion = f32[1024,1024]{1,0:T(8,128)} fusion(f32[1024,1024]{1,0:T(8,128)} %fusion.2, bf16[512,1024]{1,0:T(8,128)(2,1)} %param.25, bf16[1024,4096]{1,0:T(8,128)(2,1)} %bitcast.131, s32[]{:T(128)S(6)} %select_n.46), kind=kOutput, calls=%fused_computation.7 | convolution fusion | flops 1074790400 | bytes 10485764 | tf_op jit(solution)/shard_map/dot_general | solution.py:21
  111.3 1.7 fusion.18
  114.2 2.6 copy.56
  117.2 6.5 %multiply_reduce_fusion.8 = (f32[128]{0:T(128)S(1)}, f32[1,128,32,64]{1,3,2,0:T(8,128)}) fusion(f32[1,128,32,64]{1,3,2,0:T(8,128)} %bitcast.135, f32[32]{0:T(128)S(1)} %copy-done.32, f32[128,32,64]{0,2,1:T(8,128)} %bitcast.136, f32[128,32]{0,1:T(8,128)S(1)} %copy.59, f32[128,32]{0,1:T(8,128)S(1)} %copy.54, f32[128,128]{1,0:T(8,128)S(1)} %fusion.45, ...), kind=kOutput, calls=%fused_computation.55 | convolution fusion | flops 405798784 | bytes 3261056 | tf_op jit(solution)/shard_map/vmap(jvp(tsh,shp->thp))/dot_general | solution.py:51
  123.7 1.6 copy.61
  125.3 65.9 %all-reduce.19.cloned.1.call-done = f32[8,128,1024]{2,1,0:T(8,128)} async-done(((f32[8,128,1024]{2,1,0:T(8,128)}), f32[8,128,1024]{2,1,0:T(8,128)}) %all-reduce.19.cloned.1.call-update) | async-done | bytes 4194320 | tf_op jit(solution)/shard_map/psum | solution.py:123
  191.1 3.2 fusion.19
  194.7 2.2 multiply_reduce_fusion.6
  198.3 2.6 copy.64
  200.9 6.2 %fusion.12 = (f32[128,32]{0,1:T(8,128)S(1)}, f32[128,32]{0,1:T(8,128)S(1)}, f32[128,32]{0,1:T(8,128)S(1)}, f32[128,128]{1,0:T(8,128)S(1)}) fusion(f32[128,32]{0,1:T(8,128)S(1)} %copy.59, f32[128,32]{0,1:T(8,128)S(1)} %copy.54, f32[128,128]{1,0:T(8,128)S(1)} %fusion.45, pred[128,128]{1,0:T(8,128)(4,1)S(1)} %iota_compare_fusion, ...), kind=kOutput, calls=%fused_computation.26 | convolution fusion | flops 409440256 | bytes 2326528 | tf_op jit(solution)/shard_map/vmap(transpose(jvp(tsh,shp->thp)))/dot_general | solution.py:51
  209.5 4.1 fusion.9
  213.7 2.7 copy.68
  217.6 3.2 multiply_reduce_fusion.4
  222.3 1.7 fusion.40
  224.5 4.5 fusion.58
  229.8 39.9 %all-reduce.16 = (f32[4,2304]{1,0:T(4,128)S(1)}, f32[2048]{0:T(1024)S(1)}) all-reduce(f32[4,2304]{1,0:T(4,128)S(1)} %add_bitcast_fusion, f32[2048]{0:T(1024)S(1)} %copy-done.18), channel_id=3, replica_groups=mesh['series'=4,'head'=8] {'series','head'}, use_global_device_ids=true, to_apply=%region_16.17.clone | all-reduce | flops 11264 | bytes 90112
  270.9 50.3 %reduce-scatter.4.cloned.1.call-done = f32[32,288]{1,0:T(8,128)} async-done(((f32[1024,288]{1,0:T(8,128)}), f32[32,288]{1,0:T(8,128)}) %reduce-scatter.4.cloned.1.call-update) | async-done | bytes 36880 | tf_op jit(solution)/shard_map/reduce_scatter | solution.py:153
  321.2 150.5 %reduce-scatter.6.cloned.1.call-done = f32[64,1024]{1,0:T(8,128)} async-done(((f32[2048,1024]{1,0:T(8,128)}), f32[64,1024]{1,0:T(8,128)}) %reduce-scatter.6.cloned.1.call-update) | async-done | bytes 262160 | tf_op jit(solution)/shard_map/reduce_scatter | solution.py:156
  (114 shorter events, 16.6 us)
Async XLA Ops:
  7.2 78.4 %copy-start = (bf16[1024,1024]{1,0:T(8,128)(2,1)S(1)}, bf16[1024,1024]{1,0:T(8,128)(2,1)}, u32[]{:S(2)}) copy-start(bf16[1024,1024]{1,0:T(8,128)(2,1)} %param.24) | copy-start | bytes 6291460
  7.2 4.8 %copy-start.8 = (bf16[1,128,1024]{2,1,0:T(8,128)(2,1)S(1)}, bf16[1,128,1024]{2,1,0:T(8,128)(2,1)}, u32[]{:S(2)}) copy-start(bf16[1,128,1024]{2,1,0:T(8,128)(2,1)} %param.27) | copy-start | bytes 786436
  7.2 5.0 %copy-start.20 = (f32[1024]{0:T(1024)S(1)}, f32[1024]{0:T(1024)}, u32[]{:S(2)}) copy-start(f32[1024]{0:T(1024)} %param.31) | copy-start | bytes 12292
  7.2 5.0 %copy-start.30 = (bf16[1024,288]{0,1:T(8,128)(2,1)S(1)}, bf16[1024,288]{0,1:T(8,128)(2,1)}, u32[]{:S(2)}) copy-start(bf16[1024,288]{0,1:T(8,128)(2,1)} %param.33) | copy-start | bytes 1769476
  7.2 59.8 %all-gather.2.cloned.1.call-start = ((), (), s32[]{:S(2)}) async-start(), calls=%async_computation.2 | async-start | bytes 9437184 | tf_op jit(solution)/shard_map/all_gather | solution.py:118
  7.9 4.6 copy-start.31
  8.0 5.8 %copy-start.24 = (f32[32]{0:T(128)S(1)}, f32[32]{0:T(128)}, u32[]{:S(2)}) copy-start(f32[32]{0:T(128)} %param.35) | copy-start | bytes 388
  8.0 183.2 %all-reduce.19.cloned.1.call-start = ((), (), s32[]{:S(2)}) async-start(), calls=%async_computation.3 | async-start | bytes 8388608 | tf_op jit(solution)/shard_map/psum | solution.py:123
  16.8 94.4 %copy-start.4 = (f32[1,128,2048]{2,1,0:T(8,128)}, f32[1,128,2048]{2,1,0:T(8,128)S(1)}, u32[]{:S(2)}) copy-start(f32[1,128,2048]{2,1,0:T(8,128)S(1)} %convolution_bitcast_fusion) | copy-start | bytes 3145732
  67.1 5.8 %copy-start.3 = (bf16[8,128,4096]{2,1,0:T(8,128)(2,1)S(1)}, bf16[8,128,4096]{2,1,0:T(8,128)(2,1)}, u32[]{:S(2)}) copy-start(bf16[8,128,4096]{2,1,0:T(8,128)(2,1)} %all-gather.2.cloned.1.call-done) | copy-start | bytes 25165828
  110.0 211.3 %reduce-scatter.4.cloned.1.call-start = ((), (), s32[]{:S(2)}) async-start(), calls=%async_computation.4 | async-start | bytes 1622016 | tf_op jit(solution)/shard_map/reduce_scatter | solution.py:153
  113.0 3.9 copy-start.6
  113.0 4.2 copy-start.32
  116.9 84.0 %copy-start.19 = (pred[128,128]{1,0:T(8,128)(4,1)}, pred[128,128]{1,0:T(8,128)(4,1)S(1)}, u32[]{:S(2)}) copy-start(pred[128,128]{1,0:T(8,128)(4,1)S(1)} %iota_compare_fusion) | copy-start | bytes 49156
  123.7 67.5 %copy-start.13 = (f32[2048]{0:T(1024)S(1)}, f32[2048]{0:T(1024)}, u32[]{:S(2)}) copy-start(f32[2048]{0:T(1024)} %param.38) | copy-start | bytes 24580
  125.3 71.7 %copy-start.22 = (f32[128]{0:T(128)}, f32[128]{0:T(128)S(1)}, u32[]{:S(2)}) copy-start(f32[128]{0:T(128)S(1)} %fusion.47) | copy-start | bytes 1540
  191.1 3.6 copy-start.2
  198.3 2.6 copy-start.9
  200.9 8.6 %copy-start.10 = (f32[128,2048]{0,1:T(8,128)S(1)}, f32[128,2048]{0,1:T(8,128)}, u32[]{:S(2)}) copy-start(f32[128,2048]{0,1:T(8,128)} %copy.64) | copy-start | bytes 3145732
  213.7 4.0 copy-start.5
  222.3 1.8 copy-start.7
  222.3 1.8 copy-start.23
  224.0 247.8 %reduce-scatter.6.cloned.1.call-start = ((), (), s32[]{:S(2)}) async-start(), calls=%async_computation.5 | async-start | bytes 8650752 | tf_op jit(solution)/shard_map/reduce_scatter | solution.py:156
  229.0 242.8 %copy-start.1 = (bf16[1024,1024]{1,0:T(8,128)(2,1)S(1)}, bf16[1024,1024]{1,0:T(8,128)(2,1)}, u32[]{:S(2)}) copy-start(bf16[1024,1024]{1,0:T(8,128)(2,1)} %param.24) | copy-start | bytes 6291460
  (13 other events, 10.3 us)
Sparse Core Ops, SparseCore 0:
  9.9 57.0 all-gather.1
  110.1 80.9 all-reduce.18
  224.1 97.0 reduce-scatter.3
  324.1 147.6 reduce-scatter.5
where the time goes:
time: 479 us; the launch traced here: 478 us
  waiting for transfers between devices  318 us (66%)
  matrix products  74.8 us (16%)
  blocking collectives  39.9 us (8%)
  local copies, waits for them, and re-layouts  16.8 us (4%)
  between operations  14.8 us (3%)
  other arithmetic  13.9 us (3%)
    reduce_scatter x1, waiting for transfers between devices, per_device(): lax.psum_scatter(g_out, ('series', 'head'), scatter_dimension=0, tiled=True)  151 us
    psum x1, waiting for transfers between devices, per_device(): summed = lax.psum(group_terms, 'head')  65.9 us
    reduce_scatter x1, waiting for transfers between devices, per_device(): lax.psum_scatter(g_bcdt, ('series', 'head'), scatter_dimension=0, tiled=T...  50.3 us
    all_gather x1, waiting for transfers between devices, per_device(): row_block = lax.all_gather(teacher_in, 'head', axis=0, tiled=True)  50.2 us
    unnamed x1, blocking collectives  39.9 us
    dot_general x1, matrix products, teacher_rows(): jnp.dot(hidden, readout, preferred_element_type=jnp.float32)  18.4 us
    dot_general x3, matrix products, mixer_core(): jnp.einsum('tsh,shp->thp', weights, x_heads, precision=lax.Precision.HIGH...  16.8 us
    dot_general x1, matrix products, teacher_rows(): upward = jnp.dot(normed, w_up, preferred_element_type=jnp.float32)  12.7 us
  transfers between devices with their start and end apart: 4, of which 4 were waited for; matrix products, arithmetic and copies ran while one was open for 6% of the time, Pallas kernels for 0%

commit v1 on v0

--- a/solution.py
+++ b/solution.py
@@ -120,7 +120,9 @@
     flat_rows = row_block.reshape(count * seq_len, model_width)
     terms = teacher_rows(flat_rows, teacher_gain, w_gate, w_up, readout, distill_proj, feat_start)
     group_terms = terms.reshape(count, seq_len, terms.shape[1])
-    summed = lax.psum(group_terms, "head")
+    summed = group_terms
+    for hop in (1, 2, 4):
+        summed = summed + lax.ppermute(summed, "head", [(dev, dev ^ hop) for dev in range(8)])
     target = lax.dynamic_slice_in_dim(summed, lax.axis_index("head") * own_series, own_series, 0)
     selector = (
         building_ids[:, None]

time: 479 us -> 588 us (1.23)
  waiting for transfers between devices: 318 us -> 428 us
    ppermute x0 -> x3, waiting for transfers between devices: none -> 167 us  [per_device(): lax.ppermute(summed, 'head', [(dev, dev ^ hop) for dev in range(8)])]
    psum x1 -> x0, waiting for transfers between devices: 65.9 us -> none  [per_device(): summed = lax.psum(group_terms, 'head')]
    all_gather x1, waiting for transfers between devices: 50.2 us -> 59.1 us  [per_device(): row_block = lax.all_gather(teacher_in, 'head', axis=0, tiled=True)]
  transfers between devices with their start and end apart: 4 -> 6, of which waited for: 4 -> 6; matrix products, arithmetic and copies ran while one was open for 6% -> 5% of each run, Pallas kernels for 0% -> 0%
where the time goes in v1:
time: 588 us
  waiting for transfers between devices  428 us (73%)
  matrix products  70 us (12%)
  blocking collectives  39.8 us (7%)
  other arithmetic  17.6 us (3%)
  between operations  14.8 us (3%)
  local copies, waits for them, and re-layouts  14 us (2%)
    ppermute x3, waiting for transfers between devices, per_device(): lax.ppermute(summed, 'head', [(dev, dev ^ hop) for dev in range(8)])  167 us
    reduce_scatter x1, waiting for transfers between devices, per_device(): lax.psum_scatter(g_out, ('series', 'head'), scatter_dimension=0, tiled=True)  151 us
    all_gather x1, waiting for transfers between devices, per_device(): row_block = lax.all_gather(teacher_in, 'head', axis=0, tiled=True)  59.1 us
    reduce_scatter x1, waiting for transfers between devices, per_device(): lax.psum_scatter(g_bcdt, ('series', 'head'), scatter_dimension=0, tiled=T...  50.7 us
    unnamed x1, blocking collectives  39.8 us
    dot_general x1, matrix products, teacher_rows(): jnp.dot(hidden, readout, preferred_element_type=jnp.float32)  18.4 us
    dot_general x3, matrix products, mixer_core(): jnp.einsum('tsh,shp->thp', weights, x_heads, precision=lax.Precision.HIGH...  16 us
    dot_general x1, matrix products, teacher_rows(): upward = jnp.dot(normed, w_up, preferred_element_type=jnp.float32)  12.7 us
  transfers between devices with their start and end apart: 6, of which 6 were waited for; matrix products, arithmetic and copies ran while one was open for 5% of the time, Pallas kernels for 0%

profile of v1, /device:TPU:0, one launch (start us, length us, event | category | flops | bytes accessed | tf_op | source)
XLA Modules:
  0.0 587.9 jit_solution(12139573792179437848)
XLA Ops:
  8.0 59.1 %all-gather.2.cloned.1.call-done = bf16[8,128,4096]{2,1,0:T(8,128)(2,1)} async-done(((bf16[1,128,4096]{2,1,0:T(8,128)(2,1)}), bf16[8,128,4096]{2,1,0:T(8,128)(2,1)}) %all-gather.2.cloned.1.call-update) | async-done | bytes 8388624 | tf_op jit(solution)/shard_map/all_gather | solution.py:118
  67.0 5.2 multiply_reduce_fusion
  72.8 12.7 %fusion = f32[1024,1024]{1,0:T(8,128)} fusion(bf16[4096,1024]{1,0:T(8,128)(2,1)} %param.23, bf16[1024,4096]{1,0:T(8,128)(2,1)S(1)} %bitcast.129, f32[4096]{0:T(1024)S(1)} %copy-done.19, f32[1024]{0:T(1024)S(1)} %rsqrt_bitcast_fusion), kind=kOutput, calls=%fused_computation.4 | convolution fusion | flops 8606711808 | bytes 20992000 | tf_op jit(solution)/shard_map/dot_general | solution.py:18
  85.5 18.4 %fusion.2 = f32[1024,1024]{1,0:T(8,128)} fusion(bf16[1024,1024]{1,0:T(8,128)(2,1)S(1)} %copy-done, f32[1024,1024]{1,0:T(8,128)} %fusion, bf16[4096,1024]{1,0:T(8,128)(2,1)} %param.22, bf16[1024,4096]{1,0:T(8,128)(2,1)} %bitcast.127, f32[4096]{0:T(1024)S(1)} %copy-done.19, f32[1024]{0:T(1024)S(1)} %rsqrt_bitcast_fusion), kind=kOutput, calls=%fused_computation.6 | convolution fusion | flops 10760486912 | bytes 27283456 | tf_op jit(solution)/shard_map/dot_general | solution.py:21
  103.8 3.8 convolution_add_fusion
  107.9 6.9 %collective-permute-done = f32[8,128,1024]{2,1,0:T(8,128)S(1)} collective-permute-done((f32[8,128,1024]{2,1,0:T(8,128)S(1)}, f32[8,128,1024]{2,1,0:T(8,128)S(1)}, u32[]{:S(2)}, u32[]{:S(2)}) %collective-permute-start) | collective-permute-done | bytes 4194336 | tf_op jit(solution)/shard_map/ppermute | solution.py:125
  117.8 91.3 %collective-permute-done.1 = f32[8,128,1024]{2,1,0:T(8,128)S(1)} collective-permute-done((f32[8,128,1024]{2,1,0:T(8,128)S(1)}, f32[8,128,1024]{2,1,0:T(8,128)S(1)}, u32[]{:S(2)}, u32[]{:S(2)}) %collective-permute-start.1) | collective-permute-done | bytes 4194336 | tf_op jit(solution)/shard_map/ppermute | solution.py:125
  209.0 2.9 add.148
  214.0 2.0 fusion.57
  217.1 3.0 convolution_bitcast_fusion
  221.2 1.8 fusion.15
  224.2 2.6 copy.56
  227.1 6.5 %multiply_reduce_fusion.8 = (f32[128]{0:T(128)S(1)}, f32[1,128,32,64]{1,3,2,0:T(8,128)}) fusion(f32[1,128,32,64]{1,3,2,0:T(8,128)} %bitcast.132, f32[32]{0:T(128)S(1)} %copy-done.21, f32[128,32,64]{0,2,1:T(8,128)} %bitcast.133, f32[128,32]{0,1:T(8,128)S(1)} %copy.59, f32[128,32]{0,1:T(8,128)S(1)} %copy.54, f32[128,128]{1,0:T(8,128)S(1)} %fusion.45, ...), kind=kOutput, calls=%fused_computation.51 | convolution fusion | flops 405798784 | bytes 3261056 | tf_op jit(solution)/shard_map/vmap(jvp(tsh,shp->thp))/dot_general | solution.py:51
  235.2 69.0 %collective-permute-done.2 = f32[8,128,1024]{2,1,0:T(8,128)} collective-permute-done((f32[8,128,1024]{2,1,0:T(8,128)}, f32[8,128,1024]{2,1,0:T(8,128)}, u32[]{:S(2)}, u32[]{:S(2)}) %collective-permute-start.2) | collective-permute-done | bytes 4194336 | tf_op jit(solution)/shard_map/ppermute | solution.py:125
  304.2 3.3 fusion.36
  310.4 2.6 copy.64
  313.1 6.1 %fusion.12 = (f32[128,32]{0,1:T(8,128)S(1)}, f32[128,32]{0,1:T(8,128)S(1)}, f32[128,32]{0,1:T(8,128)S(1)}, f32[128,128]{1,0:T(8,128)S(1)}) fusion(f32[128,32]{0,1:T(8,128)S(1)} %copy.59, f32[128,32]{0,1:T(8,128)S(1)} %copy.54, f32[128,128]{1,0:T(8,128)S(1)} %fusion.45, pred[128,128]{1,0:T(8,128)(4,1)S(1)} %iota_compare_fusion, ...), kind=kOutput, calls=%fused_computation.26 | convolution fusion | flops 409440256 | bytes 2326528 | tf_op jit(solution)/shard_map/vmap(transpose(jvp(tsh,shp->thp)))/dot_general | solution.py:51
  321.4 3.4 fusion.9
  324.8 2.6 copy.68
  328.8 2.6 multiply_reduce_fusion.4
  334.3 4.5 fusion.58
  338.9 39.8 %all-reduce.16 = (f32[4,2304]{1,0:T(4,128)S(1)}, f32[2048]{0:T(1024)S(1)}) all-reduce(f32[4,2304]{1,0:T(4,128)S(1)} %add_bitcast_fusion, f32[2048]{0:T(1024)S(1)} %get-tuple-element.11), channel_id=3, replica_groups=mesh['series'=4,'head'=8] {'series','head'}, use_global_device_ids=true, to_apply=%region_15.16.clone | all-reduce | flops 11264 | bytes 90112
  380.0 50.7 %reduce-scatter.4.cloned.1.call-done = f32[32,288]{1,0:T(8,128)} async-done(((f32[1024,288]{1,0:T(8,128)}), f32[32,288]{1,0:T(8,128)}) %reduce-scatter.4.cloned.1.call-update) | async-done | bytes 36880 | tf_op jit(solution)/shard_map/reduce_scatter | solution.py:155
  430.7 150.7 %reduce-scatter.6.cloned.1.call-done = f32[64,1024]{1,0:T(8,128)} async-done(((f32[2048,1024]{1,0:T(8,128)}), f32[64,1024]{1,0:T(8,128)}) %reduce-scatter.6.cloned.1.call-update) | async-done | bytes 262160 | tf_op jit(solution)/shard_map/reduce_scatter | solution.py:158
  (97 shorter events, 21.9 us)
Async XLA Ops:
  7.2 78.3 %copy-start = (bf16[1024,1024]{1,0:T(8,128)(2,1)S(1)}, bf16[1024,1024]{1,0:T(8,128)(2,1)}, u32[]{:S(2)}) copy-start(bf16[1024,1024]{1,0:T(8,128)(2,1)} %param.24) | copy-start | bytes 6291460
  7.2 59.8 %all-gather.2.cloned.1.call-start = ((), (), s32[]{:S(2)}) async-start(), calls=%async_computation.2 | async-start | bytes 9437184 | tf_op jit(solution)/shard_map/all_gather | solution.py:118
  7.2 65.0 %copy-start.19 = (f32[4096]{0:T(1024)S(1)}, f32[4096]{0:T(1024)}, u32[]{:S(2)}) copy-start(f32[4096]{0:T(1024)} %param.21) | copy-start | bytes 49156
  7.9 422.8 %reduce-scatter.4.cloned.1.call-start = ((), (), s32[]{:S(2)}) async-start(), calls=%async_computation.3 | async-start | bytes 1622016 | tf_op jit(solution)/shard_map/reduce_scatter | solution.py:155
  67.0 5.8 copy-start.3
  85.5 18.4 %copy-start.11 = (bf16[512,1024]{1,0:T(8,128)(2,1)S(1)}, bf16[512,1024]{1,0:T(8,128)(2,1)}, u32[]{:S(2)}) copy-start(bf16[512,1024]{1,0:T(8,128)(2,1)} %param.25) | copy-start | bytes 3145732
  107.6 7.2 %collective-permute-start = (f32[8,128,1024]{2,1,0:T(8,128)S(1)}, f32[8,128,1024]{2,1,0:T(8,128)S(1)}, u32[]{:S(2)}, u32[]{:S(2)}) collective-permute-start(f32[8,128,1024]{2,1,0:T(8,128)S(1)} %bitcast.125), channel_id=1, source_target_pairs={{0,1},{1,0},{2,3},{3,2},{4,5},{5,4},{6,7},{7,6},{8,9},{9,8},{10,11... | collective-permute-start | bytes 12582920 | tf_op jit(solution)/shard_map/ppermute | solution.py:125
  116.2 97.5 %copy-start.12 = (bf16[128,1024]{1,0:T(8,128)(2,1)S(1)}, bf16[128,1024]{1,0:T(8,128)(2,1)}, u32[]{:S(2)}) copy-start(bf16[128,1024]{1,0:T(8,128)(2,1)} %param.30) | copy-start | bytes 786436
  116.2 97.5 %copy-start.13 = (bf16[1024,128]{1,0:T(8,128)(2,1)S(1)}, bf16[1024,128]{1,0:T(8,128)(2,1)}, u32[]{:S(2)}) copy-start(bf16[1024,128]{1,0:T(8,128)(2,1)} %param.29) | copy-start | bytes 786436
  116.2 92.8 %collective-permute-start.1 = (f32[8,128,1024]{2,1,0:T(8,128)S(1)}, f32[8,128,1024]{2,1,0:T(8,128)S(1)}, u32[]{:S(2)}, u32[]{:S(2)}) collective-permute-start(f32[8,128,1024]{2,1,0:T(8,128)S(1)} %add.147), channel_id=1, source_target_pairs={{0,2},{1,3},{2,0},{3,1},{4,6},{5,7},{6,4},{7,5},{8,10},{9,11},{10,... | collective-permute-start | bytes 12582920 | tf_op jit(solution)/shard_map/ppermute | solution.py:125
  211.9 4.1 copy-start.8
  211.9 4.3 copy-start.16
  211.9 4.3 copy-start.18
  211.9 92.3 %collective-permute-start.2 = (f32[8,128,1024]{2,1,0:T(8,128)}, f32[8,128,1024]{2,1,0:T(8,128)}, u32[]{:S(2)}, u32[]{:S(2)}) collective-permute-start(f32[8,128,1024]{2,1,0:T(8,128)} %add.148), channel_id=1, source_target_pairs={{0,4},{1,5},{2,6},{3,7},{4,0},{5,1},{6,2},{7,3},{8,12},{9,13},{10,... | collective-permute-start | bytes 12582920 | tf_op jit(solution)/shard_map/ppermute | solution.py:125
  213.7 2.9 copy-start.17
  214.0 3.0 copy-start.15
  223.0 3.8 copy-start.6
  223.0 4.1 copy-start.21
  233.6 70.6 %copy-start.14 = (f32[2048]{0:T(1024)S(1)}, f32[2048]{0:T(1024)}, u32[]{:S(2)}) copy-start(f32[2048]{0:T(1024)} %param.38) | copy-start | bytes 24580
  235.2 72.3 %copy-start.2 = (bf16[2048,1024]{1,0:T(8,128)(2,1)S(1)}, bf16[2048,1024]{1,0:T(8,128)(2,1)}, u32[]{:S(2)}) copy-start(bf16[2048,1024]{1,0:T(8,128)(2,1)} %param.39) | copy-start | bytes 12582916
  313.1 8.3 %copy-start.10 = (f32[128,2048]{0,1:T(8,128)S(1)}, f32[128,2048]{0,1:T(8,128)}, u32[]{:S(2)}) copy-start(f32[128,2048]{0,1:T(8,128)} %copy.64) | copy-start | bytes 3145732
  324.8 3.9 copy-start.5
  333.6 247.8 %reduce-scatter.6.cloned.1.call-start = ((), (), s32[]{:S(2)}) async-start(), calls=%async_computation.4 | async-start | bytes 8650752 | tf_op jit(solution)/shard_map/reduce_scatter | solution.py:158
  338.8 242.6 %copy-start.1 = (bf16[1024,1024]{1,0:T(8,128)(2,1)S(1)}, bf16[1024,1024]{1,0:T(8,128)(2,1)}, u32[]{:S(2)}) copy-start(bf16[1024,1024]{1,0:T(8,128)(2,1)} %param.24) | copy-start | bytes 6291460
  (4 other events, 8.6 us)
Sparse Core Ops, SparseCore 0:
  9.9 57.0 all-gather.1
  333.7 96.9 reduce-scatter.3
  433.6 147.7 reduce-scatter.5
